TPU v7x, 32 devices: a whole 2x2x4 slice. The times are simulated.
32 devices in a mesh: row: 4 (over z), col: 8 (over y, x, core).
Axes of the slice: x: 2, y: 2, z: 4, core: 2. Of those that a mesh axis runs over, the one named last changes fastest.
Arguments:
- splat_params: float32 [10, 2097152], P(None, ('row', 'col')), as said below
- list_owner: int32 [128, 1024, 1], P(('row', 'col')), may hold values from 0 to 31; in each aligned block of 4096 rows (0 to 4095, 4096 to 8191, ..., all dimensions but the last counted through in order) at most 256 rows name the same one
- list_slot: int32 [128, 1024], P(('row', 'col')), may hold values from 0 to 65535
- list_length: int32 [128], P(('row', 'col')), may hold values from 512 to 1024, as said below
- target: float32 [4, 128, 256], P(None, ('row', 'col')), may hold values from 0 to 1
Outputs:
- rendered: float32 [4, 128, 256], P(None, ('row', 'col'))
- splat_grads: float32 [10, 2097152], P(None, ('row', 'col'))
Inputs may be any that keep to these rules, and one draw needn't show every extreme that they name: `list_owner`: within the entries of one device's tiles (aligned blocks of 4096 entries), no owner is named more than 256 times, a bound that some block reaches. `list_length`: some tile has exactly 1024 live entries; every tile has at least 512. `splat_params`: conic entries satisfy a > 0, c > 0 and b * b < a * c; opacity lies in (0, 0.02]; colours and depth lie in [0, 1].
All inputs are finite; a program needn't handle non-finite values.
Results may differ from a plain program's by a relative error of at most 0.0003.
Values sent between devices are 32-bit elements; how exact they have to be, the bound alone decides.
A program may use at most 128 MiB of HBM per device.

v0:
```python
import functools

import jax
import jax.numpy as jnp
from jax import lax
from jax.experimental import pallas as pl
from jax.experimental.pallas import tpu as pltpu
from jax.sharding import PartitionSpec as P

SIDE = 16
SB = 256
LANES = 256
CH = 10
F32 = jnp.float32
BF16 = jnp.bfloat16
NT = (((1,), (1,)), ((), ()))


def iota(shape, dim):
    return lax.broadcasted_iota(jnp.int32, shape, dim)


def split(x):
    high = x.astype(BF16)
    return high, (x - high.astype(F32)).astype(BF16)


def mm(a, b):
    return jnp.dot(a, b, preferred_element_type=F32)


def mm_nt(a, b):
    return lax.dot_general(a, b, NT, preferred_element_type=F32)


def one_hot(index, size):
    return jnp.where(iota((size, index.shape[1]), 0) == index, 1.0, 0.0).astype(BF16)


def plan_kernel(own_ref, slot_ref, req_ref, rank_ref):
    devices, cap = req_ref.shape
    entries = own_ref.shape[1]
    strict = jnp.where(iota((SB, SB), 0) < iota((SB, SB), 1), 1.0, 0.0).astype(BF16)
    carry = jnp.zeros((devices, 1), F32)
    high = jnp.zeros((devices, cap), F32)
    low = jnp.zeros((devices, cap), F32)
    for j in range(entries // SB):
        part = slice(j * SB, (j + 1) * SB)
        mine = iota((devices, SB), 0) == own_ref[:, part]
        ones = jnp.where(mine, 1.0, 0.0)
        count = mm(ones.astype(BF16), strict) + carry
        rank = jnp.sum(ones * count, axis=0, keepdims=True).astype(jnp.int32)
        carry = carry + jnp.sum(ones, axis=1, keepdims=True)
        rank_ref[:, part] = rank
        slots = slot_ref[:, part]
        places = one_hot(rank, cap)
        slot_high = (slots >> 8).astype(F32)
        slot_low = (slots & 255).astype(F32)
        high = high + mm_nt(jnp.where(mine, slot_high, 0.0).astype(BF16), places)
        low = low + mm_nt(jnp.where(mine, slot_low, 0.0).astype(BF16), places)
    req_ref[...] = (high * 256.0 + low).astype(jnp.int32)


def gather_kernel(ask_ref, table_ref, out_ref, parts_ref):
    width = table_ref.shape[1]
    rows = table_ref.shape[0] // CH

    @pl.when(pl.program_id(0) == 0)
    def _():
        for ch in range(CH):
            part = slice(ch * rows, (ch + 1) * rows)
            high, low = split(table_ref[part, :])
            parts_ref[part, :width] = high
            parts_ref[part, width:] = low

    index = ask_ref[0]
    column = one_hot(index & (width - 1), width)
    row = iota((rows, index.shape[1]), 0) == (index >> 8)
    found = mm(parts_ref[...], jnp.concatenate([column, column], axis=0))
    for ch in range(CH):
        picked = jnp.where(row, found[ch * rows : (ch + 1) * rows], 0.0)
        out_ref[0, ch : ch + 1, :] = jnp.sum(picked, axis=0, keepdims=True)


def render_kernel(
    length_ref, own_ref, rank_ref, reply_ref, target_ref, image_ref, out_ref,
    vals, grads, falloff_ref, trans_ref, high_ref, low_ref, shade_ref, before_ref, pack_ref,
):
    tile = pl.program_id(0)
    devices = reply_ref.shape[0] // CH
    cap = reply_ref.shape[1]
    slots = own_ref.shape[2]
    pixels = target_ref.shape[2]
    blocks = slots // SB
    length = length_ref[tile]
    mine = iota((devices, slots), 0) == own_ref[0]
    places = one_hot(rank_ref[0], cap)
    reply_high, reply_low = split(reply_ref[...])
    fetched = mm(reply_high, places) + mm(reply_low, places)
    vals[...] = jnp.zeros_like(vals)
    live = jnp.where(iota((1, slots), 1) < length, 1.0, 0.0)
    for ch in range(CH):
        part = slice(ch * devices, (ch + 1) * devices)
        value = jnp.sum(jnp.where(mine, fetched[part], 0.0), axis=0, keepdims=True)
        if ch == 5:
            value = value * live
        row = ch if ch < 6 else ch + 2
        vals[row : row + 1, :] = value

    strict = jnp.where(iota((SB, SB), 0) < iota((SB, SB), 1), 1.0, 0.0).astype(BF16)
    inclusive = jnp.where(iota((SB, SB), 0) <= iota((SB, SB), 1), 1.0, 0.0).astype(BF16)
    centres = iota((SIDE, SB), 0).astype(F32) + 0.5
    side_rows = pixels // SIDE

    carry = jnp.zeros((pixels, 1), F32)
    image = jnp.zeros((pixels, 8), F32)
    for blk in range(blocks):
        at = slice(blk * SB, (blk + 1) * SB)
        dx = centres - vals[0:1, at]
        dy = centres - vals[1:2, at]
        ex = 0.5 * vals[2:3, at] * dx * dx
        ey = 0.5 * vals[4:5, at] * dy * dy
        bdy = vals[3:4, at] * dy
        opacity = vals[5:6, at]
        for y in range(side_rows):
            rows = slice(y * SIDE, (y + 1) * SIDE)
            exponent = ex + ey[y : y + 1] + dx * bdy[y : y + 1]
            falloff = jnp.exp(-exponent)
            falloff_ref[rows, at] = falloff
            keep = jnp.log(1.0 - opacity * falloff)
            high, low = split(keep)
            high_ref[rows, :] = high
            low_ref[rows, :] = low
        total = mm(high_ref[...], strict) + mm(low_ref[...], strict) + carry
        last = high_ref[:, SB - 128 :].astype(F32) + low_ref[:, SB - 128 :].astype(F32)
        carry = total[:, SB - 1 : SB] + last[:, 127:128]
        trans = jnp.exp(total)
        trans_ref[:, at] = trans
        weight_high, weight_low = split(trans * (opacity * falloff_ref[:, at]))
        colour_high, colour_low = split(vals[8:16, at])
        image = image + (
            mm_nt(weight_high, colour_high)
            + mm_nt(weight_high, colour_low)
            + mm_nt(weight_low, colour_high)
        )
    rendered = jnp.transpose(image)
    image_ref[0] = rendered
    grad_image = 2.0 * (rendered - target_ref[0])
    grad_high, grad_low = split(grad_image)
    grad_wide = grad_high.astype(F32)
    grad_rest = grad_image - grad_wide
    turned = jnp.transpose(jnp.concatenate([grad_wide, grad_wide, grad_rest, grad_image], axis=0))
    turned_parts = turned.astype(BF16)
    grand_total = jnp.sum(jnp.transpose(grad_image) * image, axis=1, keepdims=True)

    spent = jnp.zeros((pixels, 1), F32)
    for blk in range(blocks):
        at = slice(blk * SB, (blk + 1) * SB)
        mean_x, mean_y = vals[0:1, at], vals[1:2, at]
        conic_a, conic_b, conic_c = vals[2:3, at], vals[3:4, at], vals[4:5, at]
        opacity = vals[5:6, at]
        dx = centres - mean_x
        dy = centres - mean_y
        colours = vals[8:16, at]
        colour_wide = colours.astype(BF16).astype(F32)
        colour_parts = jnp.concatenate(
            [colour_wide, colours - colour_wide, colour_wide, jnp.zeros_like(colours)], axis=0
        ).astype(BF16)
        shading = mm(turned_parts, colour_parts)
        shade_ref[...] = shading
        weight = trans_ref[:, at] * (opacity * falloff_ref[:, at])
        weight_high, weight_low = split(weight)
        grads[8:16, at] = (
            mm(grad_high, weight_high) + mm(grad_low, weight_high) + mm(grad_high, weight_low)
        )
        high, low = split(weight * shading)
        before = mm(high, inclusive) + mm(low, inclusive) + spent
        spent = before[:, SB - 1 : SB]
        before_ref[...] = grand_total - before
        power0 = jnp.zeros((SIDE, SB), F32)
        power1 = power0
        power2 = power0
        opaque = power0
        for y in range(side_rows):
            rows = slice(y * SIDE, (y + 1) * SIDE)
            falloff = falloff_ref[rows, at]
            alpha = opacity * falloff
            grad_alpha = trans_ref[rows, at] * shade_ref[rows, :] - before_ref[rows, :] / (
                1.0 - alpha
            )
            opaque = opaque + grad_alpha * falloff
            power = grad_alpha * alpha
            power0 = power0 - power
            moment = power * dy[y : y + 1]
            power1 = power1 - moment
            power2 = power2 - moment * dy[y : y + 1]
        across = power0 * dx
        sum_x = jnp.sum(across, axis=0, keepdims=True)
        sum_y = jnp.sum(power1, axis=0, keepdims=True)
        grads[0:1, at] = -(conic_a * sum_x + conic_b * sum_y)
        grads[1:2, at] = -(conic_c * sum_y + conic_b * sum_x)
        grads[2:3, at] = 0.5 * jnp.sum(across * dx, axis=0, keepdims=True)
        grads[3:4, at] = jnp.sum(power1 * dx, axis=0, keepdims=True)
        grads[4:5, at] = 0.5 * jnp.sum(power2, axis=0, keepdims=True)
        grads[5:6, at] = jnp.sum(opaque, axis=0, keepdims=True) * live[:, at]

    for ch in range(CH):
        part = slice(ch * devices, (ch + 1) * devices)
        row = ch if ch < 6 else ch + 2
        high, low = split(jnp.where(mine, grads[row : row + 1, :], 0.0))
        pack_ref[0, part, :] = high
        pack_ref[1, part, :] = low
    sent = mm_nt(pack_ref[0], places) + mm_nt(pack_ref[1], places)

    @pl.when(tile == 0)
    def _():
        out_ref[...] = sent

    @pl.when(tile > 0)
    def _():
        out_ref[...] += sent


def scatter_kernel(ask_ref, grad_ref, out_ref, high_ref, low_ref, sum_ref):
    step = pl.program_id(0)
    halves = sum_ref.shape[0]
    width = halves * 128
    rows = sum_ref.shape[1] // CH
    index = ask_ref[...]
    column = one_hot(index & (width - 1), width)
    tops = one_hot(index >> 8, rows)
    for ch in range(CH):
        grad = jnp.broadcast_to(grad_ref[ch : ch + 1, :], (16, index.shape[1]))
        high, low = split(grad)
        for k in range(0, rows, 16):
            part = slice(ch * rows + k, ch * rows + k + 16)
            high_ref[part, :] = tops[k : k + 16] * high
            low_ref[part, :] = tops[k : k + 16] * low
    total = mm_nt(high_ref[...], column) + mm_nt(low_ref[...], column)

    @pl.when(step == 0)
    def _():
        for k in range(halves):
            sum_ref[k] = total[:, k * 128 : (k + 1) * 128]

    @pl.when(step > 0)
    def _():
        for k in range(halves):
            sum_ref[k] += total[:, k * 128 : (k + 1) * 128]

    @pl.when(step == pl.num_programs(0) - 1)
    def _():
        for q in range(rows):
            for k in range(halves):
                at = slice((q * halves + k) * 128, (q * halves + k + 1) * 128)
                out_ref[0:8, at] = sum_ref[k, pl.ds(q, 8, stride=rows), :]
                out_ref[8:CH, at] = sum_ref[k, pl.ds(8 * rows + q, CH - 8, stride=rows), :]


def body(splat_params, list_owner, list_slot, list_length, target):
    devices = lax.axis_size(("row", "col"))
    tiles, slots = list_slot.shape
    entries = tiles * slots
    splats = splat_params.shape[1]
    pixels = target.shape[2]
    cap = 2 * entries // devices
    total = devices * cap
    width = 256
    rows = splats // width
    owners = list_owner.reshape(1, entries)
    requests, ranks = pl.pallas_call(
        plan_kernel,
        out_shape=(
            jax.ShapeDtypeStruct((devices, cap), jnp.int32),
            jax.ShapeDtypeStruct((1, entries), jnp.int32),
        ),
        name="plan",
    )(owners, list_slot.reshape(1, entries))
    asked = lax.all_to_all(requests, ("row", "col"), split_axis=0, concat_axis=0, tiled=True)
    steps = total // LANES
    table = splat_params.reshape(CH * rows, width)
    looked = pl.pallas_call(
        gather_kernel,
        grid=(steps,),
        in_specs=[
            pl.BlockSpec((1, 1, LANES), lambda i: (i, 0, 0)),
            pl.BlockSpec((CH * rows, width), lambda i: (0, 0)),
        ],
        out_specs=pl.BlockSpec((1, CH, LANES), lambda i: (i, 0, 0)),
        out_shape=jax.ShapeDtypeStruct((steps, CH, LANES), F32),
        scratch_shapes=[
            pltpu.VMEM((CH * rows, 2 * width), BF16),
        ],
        name="lookup",
    )(asked.reshape(steps, 1, LANES), table)
    per = LANES // cap
    looked = looked.reshape(steps, CH, per, cap).transpose(0, 2, 1, 3).reshape(devices, CH, cap)
    answer = lax.all_to_all(looked, ("row", "col"), split_axis=0, concat_axis=0, tiled=True)
    replies = answer.transpose(1, 0, 2).reshape(CH * devices, cap)
    targets = jnp.pad(target.transpose(1, 0, 2), ((0, 0), (0, 4), (0, 0)))
    images, outgoing = pl.pallas_call(
        render_kernel,
        grid=(tiles,),
        in_specs=[
            pl.BlockSpec(memory_space=pltpu.SMEM),
            pl.BlockSpec((1, 1, slots), lambda i: (i, 0, 0)),
            pl.BlockSpec((1, 1, slots), lambda i: (i, 0, 0)),
            pl.BlockSpec((CH * devices, cap), lambda i: (0, 0)),
            pl.BlockSpec((1, 8, pixels), lambda i: (i, 0, 0)),
        ],
        out_specs=(
            pl.BlockSpec((1, 8, pixels), lambda i: (i, 0, 0)),
            pl.BlockSpec((CH * devices, cap), lambda i: (0, 0)),
        ),
        out_shape=(
            jax.ShapeDtypeStruct((tiles, 8, pixels), F32),
            jax.ShapeDtypeStruct((CH * devices, cap), F32),
        ),
        scratch_shapes=[
            pltpu.VMEM((16, slots), F32),
            pltpu.VMEM((16, slots), F32),
            pltpu.VMEM((pixels, slots), F32),
            pltpu.VMEM((pixels, slots), F32),
            pltpu.VMEM((pixels, SB), BF16),
            pltpu.VMEM((pixels, SB), BF16),
            pltpu.VMEM((pixels, SB), F32),
            pltpu.VMEM((pixels, SB), F32),
            pltpu.VMEM((2, CH * devices, slots), BF16),
        ],
        name="render",
    )(
        list_length,
        owners.reshape(tiles, 1, slots),
        ranks.reshape(tiles, 1, slots),
        replies,
        targets,
    )
    rendered = images[:, :4].transpose(1, 0, 2)
    sending = outgoing.reshape(CH, devices, cap).transpose(1, 0, 2)
    incoming = lax.all_to_all(sending, ("row", "col"), split_axis=0, concat_axis=0, tiled=True)
    arrived = incoming.transpose(1, 0, 2).reshape(CH, total)
    chunk = min(512, total)
    splat_grads = pl.pallas_call(
        scatter_kernel,
        grid=(total // chunk,),
        in_specs=[
            pl.BlockSpec((1, chunk), lambda i: (0, i)),
            pl.BlockSpec((CH, chunk), lambda i: (0, i)),
        ],
        out_specs=pl.BlockSpec((CH, splats), lambda i: (0, 0)),
        out_shape=jax.ShapeDtypeStruct((CH, splats), F32),
        scratch_shapes=[
            pltpu.VMEM((CH * rows, chunk), BF16),
            pltpu.VMEM((CH * rows, chunk), BF16),
            pltpu.VMEM((width // 128, CH * rows, 128), F32),
        ],
        name="accumulate",
    )(asked.reshape(1, total), arrived)
    return (rendered, splat_grads)


def solution(mesh):
    in_specs = (
        P(None, ("row", "col")),
        P(("row", "col"), None, None),
        P(("row", "col"), None),
        P(("row", "col")),
        P(None, ("row", "col"), None),
    )
    out_specs = (P(None, ("row", "col"), None), P(None, ("row", "col")))
    return jax.shard_map(body, mesh=mesh, in_specs=in_specs, out_specs=out_specs, check_vma=False)
```

profile of v0, /device:TPU:5, one launch (start us, length us, event | category | flops | bytes accessed | tf_op | source)
XLA Modules:
  0.0 146.7 jit_solution(3478984865124809436)
XLA Ops:
  0.6 1.3 copy.15
  2.0 5.2 %plan.1 = (s32[32,256]{1,0:T(8,128)}, s32[1,4096]{1,0:T(1,128)}) custom-call(s32[1,4096]{1,0:T(1,128)} %bitcast.29, s32[1,4096]{1,0:T(1,128)} %bitcast.32), custom_call_target="tpu_custom_call" | custom-call | tf_op jit(solution)/shard_map/plan/pallas_call | solution.py:271
  7.2 1.4 all_to_all.12
  8.6 6.4 %all-to-all-start = ((s32[32,1,256]{2,1,0:T(1,128)}), s32[32,1,256]{2,1,0:T(1,128)S(1)}, u32[]{:S(2)}, u32[]{:S(2)}) async-start(s32[32,1,256]{2,1,0:T(1,128)} %all_to_all.12), calls=%async_computation | async-start | bytes 65536 | tf_op jit(solution)/shard_map/all_to_all | solution.py:279
  14.9 0.0 copy-start.1
  15.0 3.4 %reshape.36.table_ref = f32[2560,256]{1,0:T(8,128)} reshape(f32[10,65536]{1,0:T(8,128)} %param.5) | data formatting | bytes 5242880 | tf_op jit(solution)/shard_map/reshape | solution.py:281
  18.4 2.6 %all-to-all-done.ask_ref = s32[32,1,256]{2,1,0:T(1,128)S(1)} async-done(((s32[32,1,256]{2,1,0:T(1,128)}), s32[32,1,256]{2,1,0:T(1,128)S(1)}, u32[]{:S(2)}, u32[]{:S(2)}) %all-to-all-start) | async-done | bytes 32800 | tf_op jit(solution)/shard_map/all_to_all | solution.py:279
  21.0 0.0 copy-start
  21.0 0.6 copy-done
  21.6 31.1 %lookup.1 = f32[32,10,256]{2,1,0:T(8,128)} custom-call(s32[32,1,256]{2,1,0:T(1,128)} %copy-done, f32[2560,256]{1,0:T(8,128)} %reshape.36.table_ref), custom_call_target="tpu_custom_call" | custom-call | tf_op jit(solution)/shard_map/lookup/pallas_call | solution.py:282
  52.7 3.7 %all-to-all-start.1 = ((f32[32,10,256]{2,1,0:T(8,128)}), f32[32,10,256]{2,1,0:T(8,128)S(1)}, u32[]{:S(2)}, u32[]{:S(2)}) async-start(f32[32,10,256]{2,1,0:T(8,128)} %lookup.1), calls=%async_computation.1 | async-start | bytes 1048576 | tf_op jit(solution)/shard_map/all_to_all | solution.py:298
  56.4 0.0 copy-done.1
  56.5 0.6 pad.4.target_ref
  57.1 13.8 %all-to-all-done.1 = f32[32,10,256]{2,1,0:T(8,128)S(1)} async-done(((f32[32,10,256]{2,1,0:T(8,128)}), f32[32,10,256]{2,1,0:T(8,128)S(1)}, u32[]{:S(2)}, u32[]{:S(2)}) %all-to-all-start.1) | async-done | bytes 327712 | tf_op jit(solution)/shard_map/all_to_all | solution.py:298
  70.9 0.9 copy.10
  71.8 19.5 %render.1 = (f32[4,8,256]{2,1,0:T(8,128)}, f32[320,256]{1,0:T(8,128)}) custom-call(s32[4]{0:T(128)} %length_ref.1, s32[4,1,1024]{2,1,0:T(1,128)} %bitcast.30, s32[4,1,1024]{2,1,0:T(1,128)} %bitcast.33, f32[320,256]{1,0:T(8,128)} %bitcast.26, f32[4,8,256]{2,1,0:T(8,128)} %pad.4.target_ref), custom_call_target="tpu_custom_call" | custom-call | tf_op jit(solution)/shard_map/render/pallas_call | solution.py:301
  91.3 2.0 %copy.19 = f32[10,32,256]{2,0,1:T(8,128)} copy(f32[10,32,256]{2,1,0:T(8,128)} %bitcast.27) | data formatting | bytes 655360 | tf_op jit(solution)/shard_map/reshape | solution.py:339
  93.2 4.2 %all-to-all-start.2 = ((f32[32,10,256]{2,1,0:T(8,128)}), f32[32,10,256]{2,1,0:T(8,128)S(1)}, u32[]{:S(2)}, u32[]{:S(2)}) async-start(f32[32,10,256]{2,1,0:T(8,128)} %bitcast.20), calls=%async_computation.2 | async-start | bytes 1048576 | tf_op jit(solution)/shard_map/all_to_all | solution.py:340
  97.4 0.8 slice_bitcast_fusion
  98.2 0.6 copy.14
  98.8 12.9 %all-to-all-done.2 = f32[32,10,256]{2,1,0:T(8,128)S(1)} async-done(((f32[32,10,256]{2,1,0:T(8,128)}), f32[32,10,256]{2,1,0:T(8,128)S(1)}, u32[]{:S(2)}, u32[]{:S(2)}) %all-to-all-start.2) | async-done | bytes 327712 | tf_op jit(solution)/shard_map/all_to_all | solution.py:340
  111.7 0.2 copy.13
  112.0 1.1 copy.16
  113.1 33.7 %accumulate.1 = f32[10,65536]{1,0:T(8,128)} custom-call(s32[1,8192]{1,0:T(1,128)} %bitcast.28, f32[10,8192]{1,0:T(8,128)} %bitcast.22), custom_call_target="tpu_custom_call" | custom-call | tf_op jit(solution)/shard_map/accumulate/pallas_call | solution.py:343
  (2 shorter events, 0.0 us)
Async XLA Ops:
  8.6 12.4 %all-to-all-start = ((s32[32,1,256]{2,1,0:T(1,128)}), s32[32,1,256]{2,1,0:T(1,128)S(1)}, u32[]{:S(2)}, u32[]{:S(2)}) async-start(s32[32,1,256]{2,1,0:T(1,128)} %all_to_all.12), calls=%async_computation | async-start | bytes 65536 | tf_op jit(solution)/shard_map/all_to_all | solution.py:279
  14.9 41.5 %copy-start.1 = (f32[4,4,256]{2,1,0:T(4,128)S(1)}, f32[4,4,256]{2,1,0:T(4,128)}, u32[]{:S(2)}) copy-start(f32[4,4,256]{2,1,0:T(4,128)} %param.9) | copy-start | bytes 49156
  21.0 0.6 copy-start
  52.7 18.2 %all-to-all-start.1 = ((f32[32,10,256]{2,1,0:T(8,128)}), f32[32,10,256]{2,1,0:T(8,128)S(1)}, u32[]{:S(2)}, u32[]{:S(2)}) async-start(f32[32,10,256]{2,1,0:T(8,128)} %lookup.1), calls=%async_computation.1 | async-start | bytes 1048576 | tf_op jit(solution)/shard_map/all_to_all | solution.py:298
  93.2 18.5 %all-to-all-start.2 = ((f32[32,10,256]{2,1,0:T(8,128)}), f32[32,10,256]{2,1,0:T(8,128)S(1)}, u32[]{:S(2)}, u32[]{:S(2)}) async-start(f32[32,10,256]{2,1,0:T(8,128)} %bitcast.20), calls=%async_computation.2 | async-start | bytes 1048576 | tf_op jit(solution)/shard_map/all_to_all | solution.py:340
where the time goes:
time: 150 us; the launch traced here: 147 us
  Pallas kernels  89.4 us (60%)
  waiting for transfers between devices  29.4 us (20%)
  starting transfers between devices  14.3 us (10%)
  local copies, waits for them, and re-layouts  12.9 us (9%)
    pallas_call x1, Pallas kernels, body(): pl.pallas_call(scatter_kernel, grid=(total // chunk,), in_specs=[pl.Block...  33.7 us
    pallas_call x1, Pallas kernels, body(): pl.pallas_call(gather_kernel, grid=(steps,), in_specs=[pl.BlockSpec((1, 1...  31.1 us
    pallas_call x1, Pallas kernels, body(): pl.pallas_call(render_kernel, grid=(tiles,), in_specs=[pl.BlockSpec(memor...  19.5 us
    all_to_all x1, waiting for transfers between devices, body(): lax.all_to_all(looked, ('row', 'col'), split_axis=0, concat_axis=0, tiled...  13.8 us
    all_to_all x1, waiting for transfers between devices, body(): lax.all_to_all(sending, ('row', 'col'), split_axis=0, concat_axis=0, tile...  12.9 us
    all_to_all x1, starting transfers between devices, body(): lax.all_to_all(requests, ('row', 'col'), split_axis=0, concat_axis=0, til...  6.38 us
    pallas_call x1, Pallas kernels, body(): pl.pallas_call(plan_kernel, out_shape=(jax.ShapeDtypeStruct((devices, cap...  5.2 us
    all_to_all x1, starting transfers between devices, body(): lax.all_to_all(sending, ('row', 'col'), split_axis=0, concat_axis=0, tile...  4.18 us
  transfers between devices with their start and end apart: 3, of which 3 were waited for; matrix products, arithmetic and copies ran while one was open for 4% of the time, Pallas kernels for 0%

commit v1 on v0

--- a/solution.py
+++ b/solution.py
@@ -37,49 +37,82 @@
     return jnp.where(iota((size, index.shape[1]), 0) == index, 1.0, 0.0).astype(BF16)
 
 
-def plan_kernel(own_ref, slot_ref, req_ref, rank_ref):
+def plan_kernel(length_ref, own_ref, slot_ref, req_ref, rank_ref, live_ref):
     devices, cap = req_ref.shape
     entries = own_ref.shape[1]
+    slots = entries // length_ref.shape[0]
     strict = jnp.where(iota((SB, SB), 0) < iota((SB, SB), 1), 1.0, 0.0).astype(BF16)
     carry = jnp.zeros((devices, 1), F32)
     high = jnp.zeros((devices, cap), F32)
     low = jnp.zeros((devices, cap), F32)
     for j in range(entries // SB):
         part = slice(j * SB, (j + 1) * SB)
-        mine = iota((devices, SB), 0) == own_ref[:, part]
+        place = iota((1, SB), 1) + (j * SB) % slots
+        owner = jnp.where(place < length_ref[j * SB // slots], own_ref[:, part], -1)
+        live_ref[:, part] = owner
+        mine = iota((devices, SB), 0) == owner
         ones = jnp.where(mine, 1.0, 0.0)
         count = mm(ones.astype(BF16), strict) + carry
         rank = jnp.sum(ones * count, axis=0, keepdims=True).astype(jnp.int32)
         carry = carry + jnp.sum(ones, axis=1, keepdims=True)
         rank_ref[:, part] = rank
-        slots = slot_ref[:, part]
+        named = slot_ref[:, part]
         places = one_hot(rank, cap)
-        slot_high = (slots >> 8).astype(F32)
-        slot_low = (slots & 255).astype(F32)
+        slot_high = (named >> 8).astype(F32)
+        slot_low = ((named & 255) + 1).astype(F32)
         high = high + mm_nt(jnp.where(mine, slot_high, 0.0).astype(BF16), places)
         low = low + mm_nt(jnp.where(mine, slot_low, 0.0).astype(BF16), places)
-    req_ref[...] = (high * 256.0 + low).astype(jnp.int32)
-
-
-def gather_kernel(ask_ref, table_ref, out_ref, parts_ref):
-    width = table_ref.shape[1]
-    rows = table_ref.shape[0] // CH
-
-    @pl.when(pl.program_id(0) == 0)
-    def _():
-        for ch in range(CH):
-            part = slice(ch * rows, (ch + 1) * rows)
-            high, low = split(table_ref[part, :])
-            parts_ref[part, :width] = high
-            parts_ref[part, width:] = low
-
-    index = ask_ref[0]
-    column = one_hot(index & (width - 1), width)
-    row = iota((rows, index.shape[1]), 0) == (index >> 8)
-    found = mm(parts_ref[...], jnp.concatenate([column, column], axis=0))
-    for ch in range(CH):
-        picked = jnp.where(row, found[ch * rows : (ch + 1) * rows], 0.0)
-        out_ref[0, ch : ch + 1, :] = jnp.sum(picked, axis=0, keepdims=True)
+    req_ref[...] = (high * 256.0 + low).astype(jnp.int32) - 1
+
+
+def prepare_kernel(params_ref, table_ref, wide_ref):
+    rows = table_ref.shape[0]
+    block = wide_ref.shape[1]
+    wide_ref[...] = jnp.zeros_like(wide_ref)
+
+    def step(j, _):
+        for k in range(8):
+            at = pl.ds(pl.multiple_of(k * rows + j * block, block), block)
+            wide_ref[k * 16 : k * 16 + CH, :] = params_ref[:, at]
+        table_ref[pl.ds(pl.multiple_of(j * block, block), block), :] = jnp.transpose(wide_ref[...])
+        return 0
+
+    lax.fori_loop(0, rows // block, step, 0)
+
+
+def lookup_kernel(row_ref, ask_ref, table_ref, out_ref, even_ref, odd_ref):
+    rows = table_ref.shape[0]
+    width = ask_ref.shape[1]
+    steps = ask_ref.shape[0]
+    cap = out_ref.shape[2]
+    shift = rows.bit_length() - 1
+    eye = jnp.where(iota((128, 128), 0) == iota((128, 128), 1), 1.0, 0.0).astype(BF16)
+
+    def fetch(step, held):
+        for j in range(width):
+            held[j : j + 1, :] = table_ref[pl.ds(row_ref[step * width + j], 1), :]
+
+    def pick(step, held):
+        high, low = split(held[...])
+        turned = mm_nt(eye, high) + mm_nt(eye, low)
+        group = ask_ref[pl.ds(step, 1), :] >> shift
+        found = jnp.zeros((16, width), F32)
+        for k in range(8):
+            found = found + jnp.where(group == k, turned[k * 16 : k * 16 + 16], 0.0)
+        for k in range(width // cap):
+            out_ref[step * (width // cap) + k] = found[:CH, k * cap : (k + 1) * cap]
+
+    fetch(0, even_ref)
+
+    def pair(p, _):
+        step = 2 * p
+        fetch(step + 1, odd_ref)
+        pick(step, even_ref)
+        fetch(lax.rem(step + 2, steps), even_ref)
+        pick(step + 1, odd_ref)
+        return 0
+
+    lax.fori_loop(0, steps // 2, pair, 0)
 
 
 def render_kernel(
@@ -221,40 +254,61 @@
         out_ref[...] += sent
 
 
-def scatter_kernel(ask_ref, grad_ref, out_ref, high_ref, low_ref, sum_ref):
-    step = pl.program_id(0)
-    halves = sum_ref.shape[0]
-    width = halves * 128
-    rows = sum_ref.shape[1] // CH
-    index = ask_ref[...]
-    column = one_hot(index & (width - 1), width)
-    tops = one_hot(index >> 8, rows)
-    for ch in range(CH):
-        grad = jnp.broadcast_to(grad_ref[ch : ch + 1, :], (16, index.shape[1]))
-        high, low = split(grad)
-        for k in range(0, rows, 16):
-            part = slice(ch * rows + k, ch * rows + k + 16)
-            high_ref[part, :] = tops[k : k + 16] * high
-            low_ref[part, :] = tops[k : k + 16] * low
-    total = mm_nt(high_ref[...], column) + mm_nt(low_ref[...], column)
-
-    @pl.when(step == 0)
-    def _():
-        for k in range(halves):
-            sum_ref[k] = total[:, k * 128 : (k + 1) * 128]
-
-    @pl.when(step > 0)
-    def _():
-        for k in range(halves):
-            sum_ref[k] += total[:, k * 128 : (k + 1) * 128]
-
-    @pl.when(step == pl.num_programs(0) - 1)
-    def _():
-        for q in range(rows):
-            for k in range(halves):
-                at = slice((q * halves + k) * 128, (q * halves + k + 1) * 128)
-                out_ref[0:8, at] = sum_ref[k, pl.ds(q, 8, stride=rows), :]
-                out_ref[8:CH, at] = sum_ref[k, pl.ds(8 * rows + q, CH - 8, stride=rows), :]
+def scatter_kernel(row_ref, count_ref, ask_ref, grad_ref, out_ref, wide_ref, *banks):
+    rows = banks[0].shape[0]
+    devices, _, cap = grad_ref.shape
+    width = ask_ref.shape[1]
+    steps = ask_ref.shape[0]
+    shift = rows.bit_length() - 1
+    unit = 256
+
+    def clear(j, _):
+        at = pl.ds(pl.multiple_of(j * unit, unit), unit)
+        for bank in banks:
+            bank[at, :] = jnp.zeros((unit, 128), F32)
+        return 0
+
+    lax.fori_loop(0, rows // unit, clear, 0)
+
+    def widen(step, _):
+        group = ask_ref[pl.ds(step, 1), :] >> shift
+        parts = [grad_ref[step * (width // cap) + k] for k in range(width // cap)]
+        grad = jnp.concatenate(parts, axis=1) if len(parts) > 1 else parts[0]
+        grad = jnp.concatenate([grad, jnp.zeros((16 - CH, width), F32)], axis=0)
+        wide = jnp.concatenate([jnp.where(group == k, grad, 0.0) for k in range(8)], axis=0)
+        wide_ref[pl.ds(pl.multiple_of(step * width, width), width), :] = jnp.transpose(wide)
+        return 0
+
+    lax.fori_loop(0, steps, widen, 0)
+    burst = 16
+
+    def source(s, _):
+        def add(j, _):
+            base = s * cap + j * burst
+            lines = wide_ref[pl.ds(pl.multiple_of(base, burst), burst), :]
+            for u in range(burst):
+                bank = banks[u % len(banks)]
+                at = pl.ds(row_ref[base + u], 1)
+                bank[at, :] = bank[at, :] + lines[u : u + 1]
+            return 0
+
+        return lax.fori_loop(0, (count_ref[s] + burst - 1) // burst, add, 0)
+
+    lax.fori_loop(0, devices, source, 0)
+    block = 512
+
+    def finish(j, _):
+        at = pl.ds(pl.multiple_of(j * block, block), block)
+        total = banks[0][at, :]
+        for bank in banks[1:]:
+            total = total + bank[at, :]
+        turned = jnp.transpose(total)
+        for k in range(8):
+            to = pl.ds(pl.multiple_of(k * rows + j * block, block), block)
+            out_ref[:, to] = turned[k * 16 : k * 16 + CH]
+        return 0
+
+    lax.fori_loop(0, rows // block, finish, 0)
 
 
 def body(splat_params, list_owner, list_slot, list_length, target):
@@ -265,36 +319,39 @@
     pixels = target.shape[2]
     cap = 2 * entries // devices
     total = devices * cap
-    width = 256
-    rows = splats // width
+    rows = splats // 8
+    smem = pl.BlockSpec(memory_space=pltpu.SMEM)
+    vmem = pl.BlockSpec(memory_space=pltpu.VMEM)
     owners = list_owner.reshape(1, entries)
-    requests, ranks = pl.pallas_call(
+    requests, ranks, living = pl.pallas_call(
         plan_kernel,
+        in_specs=[smem, vmem, vmem],
         out_shape=(
             jax.ShapeDtypeStruct((devices, cap), jnp.int32),
             jax.ShapeDtypeStruct((1, entries), jnp.int32),
+            jax.ShapeDtypeStruct((1, entries), jnp.int32),
         ),
         name="plan",
-    )(owners, list_slot.reshape(1, entries))
+    )(list_length, owners, list_slot.reshape(1, entries))
     asked = lax.all_to_all(requests, ("row", "col"), split_axis=0, concat_axis=0, tiled=True)
+    table = pl.pallas_call(
+        prepare_kernel,
+        out_shape=jax.ShapeDtypeStruct((rows, 128), F32),
+        scratch_shapes=[pltpu.VMEM((128, 512), F32)],
+        cost_estimate=pl.CostEstimate(flops=0, bytes_accessed=8 * CH * splats, transcendentals=0),
+        name="prepare",
+    )(splat_params)
     steps = total // LANES
-    table = splat_params.reshape(CH * rows, width)
+    lines = (asked & (rows - 1)).reshape(total)
+    counts = jnp.sum((asked >= 0).astype(jnp.int32), axis=1)
+    groups = asked.reshape(steps, LANES)
     looked = pl.pallas_call(
-        gather_kernel,
-        grid=(steps,),
-        in_specs=[
-            pl.BlockSpec((1, 1, LANES), lambda i: (i, 0, 0)),
-            pl.BlockSpec((CH * rows, width), lambda i: (0, 0)),
-        ],
-        out_specs=pl.BlockSpec((1, CH, LANES), lambda i: (i, 0, 0)),
-        out_shape=jax.ShapeDtypeStruct((steps, CH, LANES), F32),
-        scratch_shapes=[
-            pltpu.VMEM((CH * rows, 2 * width), BF16),
-        ],
+        lookup_kernel,
+        in_specs=[smem, vmem, vmem],
+        out_shape=jax.ShapeDtypeStruct((devices, CH, cap), F32),
+        scratch_shapes=[pltpu.VMEM((LANES, 128), F32)] * 2,
         name="lookup",
-    )(asked.reshape(steps, 1, LANES), table)
-    per = LANES // cap
-    looked = looked.reshape(steps, CH, per, cap).transpose(0, 2, 1, 3).reshape(devices, CH, cap)
+    )(lines, groups, table)
     answer = lax.all_to_all(looked, ("row", "col"), split_axis=0, concat_axis=0, tiled=True)
     replies = answer.transpose(1, 0, 2).reshape(CH * devices, cap)
     targets = jnp.pad(target.transpose(1, 0, 2), ((0, 0), (0, 4), (0, 0)))
@@ -330,7 +387,7 @@
         name="render",
     )(
         list_length,
-        owners.reshape(tiles, 1, slots),
+        living.reshape(tiles, 1, slots),
         ranks.reshape(tiles, 1, slots),
         replies,
         targets,
@@ -338,24 +395,13 @@
     rendered = images[:, :4].transpose(1, 0, 2)
     sending = outgoing.reshape(CH, devices, cap).transpose(1, 0, 2)
     incoming = lax.all_to_all(sending, ("row", "col"), split_axis=0, concat_axis=0, tiled=True)
-    arrived = incoming.transpose(1, 0, 2).reshape(CH, total)
-    chunk = min(512, total)
     splat_grads = pl.pallas_call(
         scatter_kernel,
-        grid=(total // chunk,),
-        in_specs=[
-            pl.BlockSpec((1, chunk), lambda i: (0, i)),
-            pl.BlockSpec((CH, chunk), lambda i: (0, i)),
-        ],
-        out_specs=pl.BlockSpec((CH, splats), lambda i: (0, 0)),
+        in_specs=[smem, smem, vmem, vmem],
         out_shape=jax.ShapeDtypeStruct((CH, splats), F32),
-        scratch_shapes=[
-            pltpu.VMEM((CH * rows, chunk), BF16),
-            pltpu.VMEM((CH * rows, chunk), BF16),
-            pltpu.VMEM((width // 128, CH * rows, 128), F32),
-        ],
+        scratch_shapes=[pltpu.VMEM((total, 128), F32)] + [pltpu.VMEM((rows, 128), F32)] * 4,
         name="accumulate",
-    )(asked.reshape(1, total), arrived)
+    )(lines, counts, groups, incoming)
     return (rendered, splat_grads)
 
 

time: 150 us -> 118 us (0.79); the launches traced: 147 us -> 117 us
  Pallas kernels: 89.4 us -> 63.7 us
  local copies, waits for them, and re-layouts: 12.9 us -> 9 us
  waiting for transfers between devices: 29.4 us -> 26 us
  starting transfers between devices: 14.3 us -> 16.5 us
    pallas_call x3 -> x4, Pallas kernels: 70 us -> 44.2 us  [the longest x1 19 us: body(): pl.pallas_call(scatter_kernel, in_specs=[smem, smem, vmem, vmem], out_sha...]
    reshape x1 -> x0, local copies, waits for them, and re-layouts: 3.4 us -> none  [body(): table = splat_params.reshape(CH * rows, width)]
    all_to_all x1, waiting for transfers between devices: 2.62 us -> 0.01 us  [body(): lax.all_to_all(requests, ('row', 'col'), split_axis=0, concat_axis=0, til...]
    all_to_all x1, starting transfers between devices: 3.72 us -> 5.85 us  [body(): lax.all_to_all(looked, ('row', 'col'), split_axis=0, concat_axis=0, tiled...]
    unnamed x9 -> x8, local copies, waits for them, and re-layouts: 3.72 us -> 3.36 us
  transfers between devices with their start and end apart: 3 -> 3, of which waited for: 3 -> 2; matrix products, arithmetic and copies ran while one was open for 4% -> 2% of each run, Pallas kernels for 0% -> 6%
where the time goes in v1:
time: 118 us; the launch traced here: 117 us
  Pallas kernels  63.7 us (54%)
  waiting for transfers between devices  26 us (22%)
  starting transfers between devices  16.5 us (14%)
  local copies, waits for them, and re-layouts  9 us (8%)
  other arithmetic  1.29 us (1%)
    pallas_call x1, Pallas kernels, body(): pl.pallas_call(render_kernel, grid=(tiles,), in_specs=[pl.BlockSpec(memor...  19.5 us
    pallas_call x1, Pallas kernels, body(): pl.pallas_call(scatter_kernel, in_specs=[smem, smem, vmem, vmem], out_sha...  19 us
    all_to_all x1, waiting for transfers between devices, body(): lax.all_to_all(looked, ('row', 'col'), split_axis=0, concat_axis=0, tiled...  13.7 us
    pallas_call x1, Pallas kernels, body(): pl.pallas_call(lookup_kernel, in_specs=[smem, vmem, vmem], out_shape=jax....  13.6 us
    all_to_all x1, waiting for transfers between devices, body(): lax.all_to_all(sending, ('row', 'col'), split_axis=0, concat_axis=0, tile...  12.3 us
    pallas_call x1, Pallas kernels, body(): pl.pallas_call(prepare_kernel, out_shape=jax.ShapeDtypeStruct((rows, 128)...  6.48 us
    all_to_all x1, starting transfers between devices, body(): lax.all_to_all(requests, ('row', 'col'), split_axis=0, concat_axis=0, til...  6.38 us
    all_to_all x1, starting transfers between devices, body(): lax.all_to_all(looked, ('row', 'col'), split_axis=0, concat_axis=0, tiled...  5.85 us
  transfers between devices with their start and end apart: 3, of which 2 were waited for; matrix products, arithmetic and copies ran while one was open for 2% of the time, Pallas kernels for 6%

profile of v1, /device:TPU:5, one launch (start us, length us, event | category | flops | bytes accessed | tf_op | source)
XLA Modules:
  0.0 117.1 jit_solution(10669723381937653180)
XLA Ops:
  0.6 1.3 %copy.20 = s32[1,1,4,1024]{3,1,2,0:T(1,128)} copy(s32[1,1,4,1024]{3,2,1,0:T(4,128)} %bitcast.36) | data formatting | bytes 32768
  2.0 5.2 %plan.1 = (s32[32,256]{1,0:T(8,128)}, s32[1,4096]{1,0:T(1,128)}, s32[1,4096]{1,0:T(1,128)}) custom-call(s32[4]{0:T(128)} %length_ref.3, s32[1,4096]{1,0:T(1,128)} %bitcast.37, s32[1,4096]{1,0:T(1,128)} %bitcast.32), custom_call_target="tpu_custom_call" | custom-call | tf_op jit(solution)/shard_map/plan/pallas_call | solution.py:326
  7.2 1.4 %copy.14 = s32[32,1,256]{2,1,0:T(1,128)} copy(s32[32,1,256]{2,0,1:T(8,128)} %bitcast.33) | data formatting | bytes 65536 | tf_op jit(solution)/shard_map/all_to_all | solution.py:336
  8.5 6.4 %all-to-all-start = ((s32[32,1,256]{2,1,0:T(1,128)}), s32[32,1,256]{2,1,0:T(1,128)S(1)}, u32[]{:S(2)}, u32[]{:S(2)}) async-start(s32[32,1,256]{2,1,0:T(1,128)} %copy.14), calls=%async_computation | async-start | bytes 65536 | tf_op jit(solution)/shard_map/all_to_all | solution.py:336
  14.9 6.5 %prepare.1.table_ref = f32[8192,128]{1,0:T(8,128)} custom-call(f32[10,65536]{1,0:T(8,128)} %params_ref.1), custom_call_target="tpu_custom_call" | custom-call | bytes 5242880 | tf_op jit(solution)/shard_map/prepare/pallas_call | solution.py:337
  21.4 0.0 copy-start.1
  21.4 0.0 all-to-all-done
  21.4 0.6 broadcast_and_fusion
  22.0 0.6 copy.27
  22.7 13.6 %lookup.1 = f32[32,10,256]{2,1,0:T(8,128)} custom-call(s32[8192]{0:T(1024)} %bitcast.27, s32[32,256]{1,0:T(8,128)} %bitcast.29, f32[8192,128]{1,0:T(8,128)} %prepare.1.table_ref), custom_call_target="tpu_custom_call" | custom-call | tf_op jit(solution)/shard_map/lookup/pallas_call | solution.py:348
  36.2 5.8 %all-to-all-start.1 = ((f32[32,10,256]{2,1,0:T(8,128)}), f32[32,10,256]{2,1,0:T(8,128)S(1)}, u32[]{:S(2)}, u32[]{:S(2)}) async-start(f32[32,10,256]{2,1,0:T(8,128)} %lookup.1), calls=%async_computation.1 | async-start | bytes 1048576 | tf_op jit(solution)/shard_map/all_to_all | solution.py:355
  42.1 0.0 copy-done.1
  42.1 0.6 pad.4.target_ref
  42.7 13.7 %all-to-all-done.1 = f32[32,10,256]{2,1,0:T(8,128)S(1)} async-done(((f32[32,10,256]{2,1,0:T(8,128)}), f32[32,10,256]{2,1,0:T(8,128)S(1)}, u32[]{:S(2)}, u32[]{:S(2)}) %all-to-all-start.1) | async-done | bytes 327712 | tf_op jit(solution)/shard_map/all_to_all | solution.py:355
  56.4 0.9 copy.15
  57.3 19.5 %render.1 = (f32[4,8,256]{2,1,0:T(8,128)}, f32[320,256]{1,0:T(8,128)}) custom-call(s32[4]{0:T(128)} %length_ref.3, s32[4,1,1024]{2,1,0:T(1,128)} %bitcast.35, s32[4,1,1024]{2,1,0:T(1,128)} %bitcast.34, f32[320,256]{1,0:T(8,128)} %bitcast.25, f32[4,8,256]{2,1,0:T(8,128)} %pad.4.target_ref), custom_call_target="tpu_custom_call" | custom-call | tf_op jit(solution)/shard_map/render/pallas_call | solution.py:358
  76.8 2.0 %copy.26 = f32[10,32,256]{2,0,1:T(8,128)} copy(f32[10,32,256]{2,1,0:T(8,128)} %bitcast.26) | data formatting | bytes 655360 | tf_op jit(solution)/shard_map/reshape | solution.py:396
  78.8 4.3 %all-to-all-start.2 = ((f32[32,10,256]{2,1,0:T(8,128)}), f32[32,10,256]{2,1,0:T(8,128)S(1)}, u32[]{:S(2)}, u32[]{:S(2)}) async-start(f32[32,10,256]{2,1,0:T(8,128)} %bitcast.21), calls=%async_computation.2 | async-start | bytes 1048576 | tf_op jit(solution)/shard_map/all_to_all | solution.py:397
  83.0 0.7 convert_reduce_fusion.count_ref
  83.7 0.8 slice_bitcast_fusion
  84.4 0.6 copy.18
  85.1 12.3 %all-to-all-done.2.grad_ref = f32[32,10,256]{2,1,0:T(8,128)S(1)} async-done(((f32[32,10,256]{2,1,0:T(8,128)}), f32[32,10,256]{2,1,0:T(8,128)S(1)}, u32[]{:S(2)}, u32[]{:S(2)}) %all-to-all-start.2) | async-done | bytes 327712 | tf_op jit(solution)/shard_map/all_to_all | solution.py:397
  97.4 0.8 copy-done
  98.1 19.0 %accumulate.1 = f32[10,65536]{1,0:T(8,128)} custom-call(s32[8192]{0:T(1024)} %bitcast.28, s32[32]{0:T(128)} %convert_reduce_fusion.count_ref, s32[32,256]{1,0:T(8,128)} %bitcast.30, f32[32,10,256]{2,1,0:T(8,128)} %copy-done), custom_call_target="tpu_custom_call" | custom-call | tf_op jit(solution)/shard_map/accumulate/pallas_call | solution.py:398
  (2 shorter events, 0.0 us)
Async XLA Ops:
  8.5 12.9 %all-to-all-start = ((s32[32,1,256]{2,1,0:T(1,128)}), s32[32,1,256]{2,1,0:T(1,128)S(1)}, u32[]{:S(2)}, u32[]{:S(2)}) async-start(s32[32,1,256]{2,1,0:T(1,128)} %copy.14), calls=%async_computation | async-start | bytes 65536 | tf_op jit(solution)/shard_map/all_to_all | solution.py:336
  21.4 20.7 %copy-start.1 = (f32[4,4,256]{2,1,0:T(4,128)S(1)}, f32[4,4,256]{2,1,0:T(4,128)}, u32[]{:S(2)}) copy-start(f32[4,4,256]{2,1,0:T(4,128)} %param.9) | copy-start | bytes 49156
  36.2 20.2 %all-to-all-start.1 = ((f32[32,10,256]{2,1,0:T(8,128)}), f32[32,10,256]{2,1,0:T(8,128)S(1)}, u32[]{:S(2)}, u32[]{:S(2)}) async-start(f32[32,10,256]{2,1,0:T(8,128)} %lookup.1), calls=%async_computation.1 | async-start | bytes 1048576 | tf_op jit(solution)/shard_map/all_to_all | solution.py:355
  78.8 18.6 %all-to-all-start.2 = ((f32[32,10,256]{2,1,0:T(8,128)}), f32[32,10,256]{2,1,0:T(8,128)S(1)}, u32[]{:S(2)}, u32[]{:S(2)}) async-start(f32[32,10,256]{2,1,0:T(8,128)} %bitcast.21), calls=%async_computation.2 | async-start | bytes 1048576 | tf_op jit(solution)/shard_map/all_to_all | solution.py:397
  97.4 0.8 copy-start

commit v2 on v1

v2 whole, which is shorter than its diff:
```python
import functools

import jax
import jax.numpy as jnp
from jax import lax
from jax.experimental import pallas as pl
from jax.experimental.pallas import tpu as pltpu
from jax.sharding import PartitionSpec as P

SIDE = 16
SB = 256
LANES = 256
CH = 10
F32 = jnp.float32
BF16 = jnp.bfloat16
NT = (((1,), (1,)), ((), ()))


def iota(shape, dim):
    return lax.broadcasted_iota(jnp.int32, shape, dim)


def split(x):
    high = x.astype(BF16)
    return high, (x - high.astype(F32)).astype(BF16)


def mm(a, b):
    return jnp.dot(a, b, preferred_element_type=F32)


def mm_nt(a, b):
    return lax.dot_general(a, b, NT, preferred_element_type=F32)


def one_hot(index, size):
    return jnp.where(iota((size, index.shape[1]), 0) == index, 1.0, 0.0).astype(BF16)


def step_kernel(
    length_ref, own_ref, slot_ref, target_ref, params_hbm, image_ref, asked_ref, incoming_ref,
    params_ref, table_ref, wide_ref, even_ref, odd_ref, lines_ref, live_ref, rank_ref, req_ref,
    found_ref, replies_ref, outgoing_ref, reply_high, reply_low, sent_ref,
    vals, grads, falloff_ref, trans_ref, high_ref, low_ref, shade_ref, before_ref, pack_ref,
    local_sem, send_sem, recv_sem,
):
    rows_on = lax.axis_size("row")
    cols_on = lax.axis_size("col")
    devices = rows_on * cols_on
    me = lax.axis_index("row") * cols_on + lax.axis_index("col")
    tiles, slots = slot_ref.shape
    cap = found_ref.shape[2]
    pixels = target_ref.shape[2]
    rows = table_ref.shape[0]
    shift = rows.bit_length() - 1
    others = pl.ds(0, devices - 1)

    def peer(k):
        return lax.rem(me + k, devices)

    def place_of(device):
        return (device // cols_on, lax.rem(device, cols_on))

    def push(device, source, target, phase):
        return pltpu.make_async_remote_copy(
            src_ref=source.at[device],
            dst_ref=target.at[me],
            send_sem=send_sem.at[phase],
            recv_sem=recv_sem.at[phase],
            device_id=place_of(device),
            device_id_type=pl.DeviceIdType.MESH,
        )

    def drain(source, target, phase):
        pltpu.make_async_copy(target.at[others], target.at[others], recv_sem.at[phase]).wait()
        pltpu.make_async_copy(source.at[others], source.at[others], send_sem.at[phase]).wait()

    barrier = pltpu.get_barrier_semaphore()

    @pl.loop(1, devices)
    def _(k):
        pl.semaphore_signal(
            barrier, inc=1, device_id=place_of(peer(k)), device_id_type=pl.DeviceIdType.MESH
        )

    load = pltpu.make_async_copy(params_hbm, params_ref, local_sem.at[0])
    load.start()

    strict = jnp.where(iota((SB, SB), 0) < iota((SB, SB), 1), 1.0, 0.0).astype(BF16)
    inclusive = jnp.where(iota((SB, SB), 0) <= iota((SB, SB), 1), 1.0, 0.0).astype(BF16)
    count = jnp.zeros((devices, 1), F32)
    high = jnp.zeros((devices, cap), F32)
    low = jnp.zeros((devices, cap), F32)
    for tile in range(tiles):
        for j in range(slots // SB):
            part = slice(j * SB, (j + 1) * SB)
            owner = jnp.where(iota((1, SB), 1) + j * SB < length_ref[tile], own_ref[tile, :, part], -1)
            live_ref[tile, :, part] = owner
            mine = iota((devices, SB), 0) == owner
            ones = jnp.where(mine, 1.0, 0.0)
            ahead = mm(ones.astype(BF16), strict) + count
            rank = jnp.sum(ones * ahead, axis=0, keepdims=True).astype(jnp.int32)
            count = count + jnp.sum(ones, axis=1, keepdims=True)
            rank_ref[tile, :, part] = rank
            named = slot_ref[tile : tile + 1, part]
            places = one_hot(rank, cap)
            slot_high = (named >> 8).astype(F32)
            slot_low = ((named & 255) + 1).astype(F32)
            high = high + mm_nt(jnp.where(mine, slot_high, 0.0).astype(BF16), places)
            low = low + mm_nt(jnp.where(mine, slot_low, 0.0).astype(BF16), places)
    wanted = (high * 256.0 + low).astype(jnp.int32) - 1
    line = wanted & (rows - 1)
    group = wanted >> shift
    for d in range(devices):
        req_ref[d, :, :cap] = line[d : d + 1]
        req_ref[d, :, cap:] = group[d : d + 1]
    pl.semaphore_wait(barrier, devices - 1)

    @pl.loop(1, devices)
    def _(k):
        push(peer(k), req_ref, asked_ref, 0).start()

    asked_ref[me] = req_ref[me]
    load.wait()
    wide_ref[...] = jnp.zeros_like(wide_ref)
    block = wide_ref.shape[1]

    @pl.loop(0, rows // block)
    def _(j):
        for k in range(8):
            at = pl.ds(pl.multiple_of(k * rows + j * block, block), block)
            wide_ref[k * 16 : k * 16 + CH, :] = params_ref[:, at]
        table_ref[pl.ds(pl.multiple_of(j * block, block), block), :] = jnp.transpose(wide_ref[...])

    drain(req_ref, asked_ref, 0)
    move = pltpu.make_async_copy(asked_ref, lines_ref, local_sem.at[1])
    move.start()
    move.wait()

    eye = jnp.where(iota((128, 128), 0) == iota((128, 128), 1), 1.0, 0.0).astype(BF16)

    def fetch(k, held):
        source = peer(k)
        for j in range(cap):
            held[j : j + 1, :] = table_ref[pl.ds(lines_ref[source, 0, j], 1), :]

    def pick(k, held):
        source = peer(k)
        high, low = split(held[...])
        turned = mm_nt(eye, high) + mm_nt(eye, low)
        group = asked_ref[source, :, cap:]
        found = jnp.zeros((16, cap), F32)
        for q in range(8):
            found = found + jnp.where(group == q, turned[q * 16 : q * 16 + 16], 0.0)
        return found[:CH]

    def answer(k, held):
        source = peer(k)
        found_ref[source] = pick(k, held)
        push(source, found_ref, replies_ref, 1).start()

    fetch(1, even_ref)

    @pl.loop(0, devices // 2 - 1)
    def _(p):
        fetch(2 * p + 2, odd_ref)
        answer(2 * p + 1, even_ref)
        fetch(2 * p + 3, even_ref)
        answer(2 * p + 2, odd_ref)

    answer(devices - 1, even_ref)
    fetch(0, odd_ref)
    replies_ref[me] = pick(0, odd_ref)
    drain(found_ref, replies_ref, 1)

    for ch in range(CH):
        part = slice(ch * devices, (ch + 1) * devices)
        reply_high[part, :], reply_low[part, :] = split(replies_ref[:, ch, :])
    sent_ref[...] = jnp.zeros_like(sent_ref)
    blocks = slots // SB
    centres = iota((SIDE, SB), 0).astype(F32) + 0.5
    side_rows = pixels // SIDE

    @pl.loop(0, tiles)
    def _(tile):
        length = length_ref[tile]
        mine = iota((devices, slots), 0) == live_ref[tile]
        places = one_hot(rank_ref[tile], cap)
        fetched = mm(reply_high[...], places) + mm(reply_low[...], places)
        vals[...] = jnp.zeros_like(vals)
        live = jnp.where(iota((1, slots), 1) < length, 1.0, 0.0)
        for ch in range(CH):
            part = slice(ch * devices, (ch + 1) * devices)
            value = jnp.sum(jnp.where(mine, fetched[part], 0.0), axis=0, keepdims=True)
            if ch == 5:
                value = value * live
            row = ch if ch < 6 else ch + 2
            vals[row : row + 1, :] = value

        carry = jnp.zeros((pixels, 1), F32)
        image = jnp.zeros((pixels, 8), F32)
        for blk in range(blocks):
            at = slice(blk * SB, (blk + 1) * SB)
            dx = centres - vals[0:1, at]
            dy = centres - vals[1:2, at]
            ex = 0.5 * vals[2:3, at] * dx * dx
            ey = 0.5 * vals[4:5, at] * dy * dy
            bdy = vals[3:4, at] * dy
            opacity = vals[5:6, at]
            for y in range(side_rows):
                rows = slice(y * SIDE, (y + 1) * SIDE)
                exponent = ex + ey[y : y + 1] + dx * bdy[y : y + 1]
                falloff = jnp.exp(-exponent)
                falloff_ref[rows, at] = falloff
                keep = jnp.log(1.0 - opacity * falloff)
                high, low = split(keep)
                high_ref[rows, :] = high
                low_ref[rows, :] = low
            total = mm(high_ref[...], strict) + mm(low_ref[...], strict) + carry
            last = high_ref[:, SB - 128 :].astype(F32) + low_ref[:, SB - 128 :].astype(F32)
            carry = total[:, SB - 1 : SB] + last[:, 127:128]
            trans = jnp.exp(total)
            trans_ref[:, at] = trans
            weight_high, weight_low = split(trans * (opacity * falloff_ref[:, at]))
            colour_high, colour_low = split(vals[8:16, at])
            image = image + (
                mm_nt(weight_high, colour_high)
                + mm_nt(weight_high, colour_low)
                + mm_nt(weight_low, colour_high)
            )
        rendered = jnp.transpose(image)
        for ch in range(4):
            image_ref[ch, pl.ds(tile, 1), :] = rendered[ch : ch + 1]
        wished = [target_ref[ch, pl.ds(tile, 1), :] for ch in range(4)]
        wished = jnp.concatenate(wished + [jnp.zeros((4, pixels), F32)], axis=0)
        grad_image = 2.0 * (rendered - wished)
        grad_high, grad_low = split(grad_image)
        grad_wide = grad_high.astype(F32)
        grad_rest = grad_image - grad_wide
        turned = jnp.transpose(jnp.concatenate([grad_wide, grad_wide, grad_rest, grad_image], axis=0))
        turned_parts = turned.astype(BF16)
        grand_total = jnp.sum(jnp.transpose(grad_image) * image, axis=1, keepdims=True)

        spent = jnp.zeros((pixels, 1), F32)
        for blk in range(blocks):
            at = slice(blk * SB, (blk + 1) * SB)
            mean_x, mean_y = vals[0:1, at], vals[1:2, at]
            conic_a, conic_b, conic_c = vals[2:3, at], vals[3:4, at], vals[4:5, at]
            opacity = vals[5:6, at]
            dx = centres - mean_x
            dy = centres - mean_y
            colours = vals[8:16, at]
            colour_wide = colours.astype(BF16).astype(F32)
            colour_parts = jnp.concatenate(
                [colour_wide, colours - colour_wide, colour_wide, jnp.zeros_like(colours)], axis=0
            ).astype(BF16)
            shading = mm(turned_parts, colour_parts)
            shade_ref[...] = shading
            weight = trans_ref[:, at] * (opacity * falloff_ref[:, at])
            weight_high, weight_low = split(weight)
            grads[8:16, at] = (
                mm(grad_high, weight_high) + mm(grad_low, weight_high) + mm(grad_high, weight_low)
            )
            high, low = split(weight * shading)
            before = mm(high, inclusive) + mm(low, inclusive) + spent
            spent = before[:, SB - 1 : SB]
            before_ref[...] = grand_total - before
            power0 = jnp.zeros((SIDE, SB), F32)
            power1 = power0
            power2 = power0
            opaque = power0
            for y in range(side_rows):
                rows = slice(y * SIDE, (y + 1) * SIDE)
                falloff = falloff_ref[rows, at]
                alpha = opacity * falloff
                grad_alpha = trans_ref[rows, at] * shade_ref[rows, :] - before_ref[rows, :] / (
                    1.0 - alpha
                )
                opaque = opaque + grad_alpha * falloff
                power = grad_alpha * alpha
                power0 = power0 - power
                moment = power * dy[y : y + 1]
                power1 = power1 - moment
                power2 = power2 - moment * dy[y : y + 1]
            across = power0 * dx
            sum_x = jnp.sum(across, axis=0, keepdims=True)
            sum_y = jnp.sum(power1, axis=0, keepdims=True)
            grads[0:1, at] = -(conic_a * sum_x + conic_b * sum_y)
            grads[1:2, at] = -(conic_c * sum_y + conic_b * sum_x)
            grads[2:3, at] = 0.5 * jnp.sum(across * dx, axis=0, keepdims=True)
            grads[3:4, at] = jnp.sum(power1 * dx, axis=0, keepdims=True)
            grads[4:5, at] = 0.5 * jnp.sum(power2, axis=0, keepdims=True)
            grads[5:6, at] = jnp.sum(opaque, axis=0, keepdims=True) * live[:, at]

        for ch in range(CH):
            part = slice(ch * devices, (ch + 1) * devices)
            row = ch if ch < 6 else ch + 2
            high, low = split(jnp.where(mine, grads[row : row + 1, :], 0.0))
            pack_ref[0, part, :] = high
            pack_ref[1, part, :] = low
        sent = mm_nt(pack_ref[0], places) + mm_nt(pack_ref[1], places)

        sent_ref[...] += sent

    for ch in range(CH):
        part = slice(ch * devices, (ch + 1) * devices)
        outgoing_ref[:, ch, :] = sent_ref[part, :]

    @pl.loop(1, devices)
    def _(k):
        push(peer(k), outgoing_ref, incoming_ref, 2).start()

    incoming_ref[me] = outgoing_ref[me]
    drain(outgoing_ref, incoming_ref, 2)


def scatter_kernel(row_ref, count_ref, ask_ref, grad_ref, out_ref, wide_ref, *banks):
    rows = banks[0].shape[0]
    devices, _, cap = grad_ref.shape
    width = ask_ref.shape[1]
    steps = ask_ref.shape[0]
    unit = 256

    def clear(j, _):
        at = pl.ds(pl.multiple_of(j * unit, unit), unit)
        for bank in banks:
            bank[at, :] = jnp.zeros((unit, 128), F32)
        return 0

    lax.fori_loop(0, rows // unit, clear, 0)

    def widen(step, _):
        group = ask_ref[pl.ds(step, 1), :]
        parts = [grad_ref[step * (width // cap) + k] for k in range(width // cap)]
        grad = jnp.concatenate(parts, axis=1) if len(parts) > 1 else parts[0]
        grad = jnp.concatenate([grad, jnp.zeros((16 - CH, width), F32)], axis=0)
        wide = jnp.concatenate([jnp.where(group == k, grad, 0.0) for k in range(8)], axis=0)
        wide_ref[pl.ds(pl.multiple_of(step * width, width), width), :] = jnp.transpose(wide)
        return 0

    lax.fori_loop(0, steps, widen, 0)
    burst = 16

    def source(s, _):
        def add(j, _):
            base = s * cap + j * burst
            lines = wide_ref[pl.ds(pl.multiple_of(base, burst), burst), :]
            for u in range(burst):
                bank = banks[u % len(banks)]
                at = pl.ds(row_ref[base + u], 1)
                bank[at, :] = bank[at, :] + lines[u : u + 1]
            return 0

        return lax.fori_loop(0, (count_ref[s] + burst - 1) // burst, add, 0)

    lax.fori_loop(0, devices, source, 0)
    block = 512

    def finish(j, _):
        at = pl.ds(pl.multiple_of(j * block, block), block)
        total = banks[0][at, :]
        for bank in banks[1:]:
            total = total + bank[at, :]
        turned = jnp.transpose(total)
        for k in range(8):
            to = pl.ds(pl.multiple_of(k * rows + j * block, block), block)
            out_ref[:, to] = turned[k * 16 : k * 16 + CH]
        return 0

    lax.fori_loop(0, rows // block, finish, 0)


def body(splat_params, list_owner, list_slot, list_length, target):
    devices = lax.axis_size(("row", "col"))
    tiles, slots = list_slot.shape
    entries = tiles * slots
    splats = splat_params.shape[1]
    pixels = target.shape[2]
    cap = 2 * entries // devices
    total = devices * cap
    rows = splats // 8
    smem = pl.BlockSpec(memory_space=pltpu.SMEM)
    vmem = pl.BlockSpec(memory_space=pltpu.VMEM)
    rendered, asked, incoming = pl.pallas_call(
        step_kernel,
        in_specs=[smem, vmem, vmem, vmem, pl.BlockSpec(memory_space=pl.ANY)],
        out_specs=(vmem, vmem, vmem),
        out_shape=(
            jax.ShapeDtypeStruct((4, tiles, pixels), F32),
            jax.ShapeDtypeStruct((devices, 1, 2 * cap), jnp.int32),
            jax.ShapeDtypeStruct((devices, CH, cap), F32),
        ),
        scratch_shapes=[
            pltpu.VMEM((CH, splats), F32),
            pltpu.VMEM((rows, 128), F32),
            pltpu.VMEM((128, 512), F32),
            pltpu.VMEM((cap, 128), F32),
            pltpu.VMEM((cap, 128), F32),
            pltpu.SMEM((devices, 1, 2 * cap), jnp.int32),
            pltpu.VMEM((tiles, 1, slots), jnp.int32),
            pltpu.VMEM((tiles, 1, slots), jnp.int32),
            pltpu.VMEM((devices, 1, 2 * cap), jnp.int32),
            pltpu.VMEM((devices, CH, cap), F32),
            pltpu.VMEM((devices, CH, cap), F32),
            pltpu.VMEM((devices, CH, cap), F32),
            pltpu.VMEM((CH * devices, cap), BF16),
            pltpu.VMEM((CH * devices, cap), BF16),
            pltpu.VMEM((CH * devices, cap), F32),
            pltpu.VMEM((16, slots), F32),
            pltpu.VMEM((16, slots), F32),
            pltpu.VMEM((pixels, slots), F32),
            pltpu.VMEM((pixels, slots), F32),
            pltpu.VMEM((pixels, SB), BF16),
            pltpu.VMEM((pixels, SB), BF16),
            pltpu.VMEM((pixels, SB), F32),
            pltpu.VMEM((pixels, SB), F32),
            pltpu.VMEM((2, CH * devices, slots), BF16),
            pltpu.SemaphoreType.DMA((2,)),
            pltpu.SemaphoreType.DMA((3,)),
            pltpu.SemaphoreType.DMA((3,)),
        ],
        compiler_params=pltpu.CompilerParams(collective_id=0, has_side_effects=True),
        name="step",
    )(list_length, list_owner.reshape(tiles, 1, slots), list_slot, target, splat_params)
    lines = asked[:, 0, :cap].reshape(total)
    groups = asked[:, 0, cap:]
    counts = jnp.sum((groups >= 0).astype(jnp.int32), axis=1)
    splat_grads = pl.pallas_call(
        scatter_kernel,
        in_specs=[smem, smem, vmem, vmem],
        out_shape=jax.ShapeDtypeStruct((CH, splats), F32),
        scratch_shapes=[pltpu.VMEM((total, 128), F32)] + [pltpu.VMEM((rows, 128), F32)] * 4,
        name="accumulate",
    )(lines, counts, groups.reshape(total // LANES, LANES), incoming)
    return (rendered, splat_grads)


def solution(mesh):
    in_specs = (
        P(None, ("row", "col")),
        P(("row", "col"), None, None),
        P(("row", "col"), None),
        P(("row", "col")),
        P(None, ("row", "col"), None),
    )
    out_specs = (P(None, ("row", "col"), None), P(None, ("row", "col")))
    return jax.shard_map(body, mesh=mesh, in_specs=in_specs, out_specs=out_specs, check_vma=False)
```

time: 118 us -> 84.2 us (0.71)
  the two profiles are of different devices: /device:TPU:5 before, /device:TPU:30 now
where the time goes in v2:
time: 84.2 us; the launch traced here: 83.9 us
  Pallas kernels  79.2 us (94%)
  local copies, waits for them, and re-layouts  3.42 us (4%)
    pallas_call x1, Pallas kernels, body(): pl.pallas_call(step_kernel, in_specs=[smem, vmem, vmem, vmem, pl.BlockSpe...  60.2 us
    pallas_call x1, Pallas kernels, body(): pl.pallas_call(scatter_kernel, in_specs=[smem, smem, vmem, vmem], out_sha...  19 us

profile of v2, /device:TPU:30, one launch (start us, length us, event | category | flops | bytes accessed | tf_op | source)
XLA Modules:
  0.0 83.9 jit_solution(7024373655973644692)
XLA Ops:
  0.6 60.2 %step.1 = (f32[4,4,256]{2,1,0:T(4,128)}, s32[32,1,512]{2,1,0:T(1,128)}, f32[32,10,256]{2,1,0:T(8,128)}) custom-call(s32[4]{0:T(128)} %length_ref.1, s32[4,1,1024]{2,1,0:T(1,128)} %bitcast.7, s32[4,1024]{1,0:T(4,128)} %slot_ref.1, f32[4,4,256]{2,1,0:T(4,128)} %target_ref.1, f32[10,65536]{1,0:T(8,128)} %params_hbm.1), custom_call_target="tpu_custom_call" | custom-call | tf_op jit(solution)/shard_map/step/pallas_call | solution.py:384
  60.9 0.0 copy-start
  60.9 1.4 %slice.6 = s32[32,1,256]{2,1,0:T(1,128)} slice(s32[32,1,512]{2,1,0:T(1,128)} %get-tuple-element.6), slice={[0:32], [0:1], [0:256]} | slice | bytes 65536 | tf_op jit(solution)/shard_map/slice | solution.py:425
  62.2 0.8 %copy.7 = s32[32,1,512]{2,0,1:T(8,128)S(1)} copy(s32[32,1,512]{2,1,0:T(1,128)} %get-tuple-element.6) | data formatting | bytes 131072 | tf_op jit(solution)/shard_map/step/pallas_call | solution.py:384
  63.1 0.6 convert_reduce_fusion.count_ref
  63.7 0.6 slice_bitcast_fusion.ask_ref
  64.3 19.0 %accumulate.1 = f32[10,65536]{1,0:T(8,128)} custom-call(s32[8192]{0:T(1024)} %bitcast.6, s32[32]{0:T(128)} %convert_reduce_fusion.count_ref, s32[32,256]{1,0:T(8,128)} %slice_bitcast_fusion.ask_ref, f32[32,10,256]{2,1,0:T(8,128)} %get-tuple-element.7.grad_ref), custom_call_target="tpu_custom_call" | custom-call | tf_op jit(solution)/shard_map/accumulate/pallas_call | solution.py:428
  83.3 0.0 copy-done
  83.3 0.6 copy.9
Async XLA Ops:
  60.9 22.4 %copy-start = (f32[4,4,256]{2,1,0:T(4,128)S(1)}, f32[4,4,256]{2,1,0:T(4,128)}, u32[]{:S(2)}) copy-start(f32[4,4,256]{2,1,0:T(4,128)} %get-tuple-element.10) | copy-start | bytes 49156
